TPU v7x, 512 devices: a whole 4x4x16 slice. The times are simulated.
512 devices in a mesh: wave: 128 (over y_lo, z, x), parity: 2 (over y_hi), lev: 2 (over core).
Axes of the slice: x: 4, y: 4 (y_hi: 2, y_lo: 2; y = y_hi * 2 + y_lo), z: 16, core: 2. Of those that a mesh axis runs over, the one named last changes fastest.
Arguments:
- fourier: bfloat16 [2, 1280, 256, 256], P('parity', 'wave', None, 'lev'), may hold values from -6 to 6
- legendre: bfloat16 [256, 2, 1280, 1280], P('wave', 'parity', 'lev'), may hold values from -0.15625 to 0.15625
- quad_weights: float32 [1280], P('wave'), may hold values from 0.3 to 3
- slot_wave: int32 [256], replicated, may hold values from 0 to 255, as said below
- to_modes: float32 [128, 128], replicated, may hold values from -0.5 to 0.5
- from_modes: float32 [128, 128], replicated, may hold values from -0.5 to 0.5
- mode_rates: float32 [128], replicated, may hold values from 0.1 to 10
Outputs:
- columns: bfloat16 [2, 1280, 256, 256], P('parity', 'wave', None, 'lev')
- spectral: bfloat16 [2, 1280, 65536], P('parity', 'lev', 'wave')
Inputs may be any that keep to these rules, and one draw needn't show every extreme that they name: `slot_wave`: A permutation of the wavenumbers 0 to 255; the owner with index w on wave holds slots w * 2 to (w + 1) * 2 - 1. Slots 2 i and 2 i + 1 hold a wavenumber below 128 and 255 minus it, in that order.
All inputs are finite; a program needn't handle non-finite values.
Results may differ from a plain program's by a relative error of at most 0.014.
Values may be sent and summed in bfloat16 or wider, within the bound.
A program may use at most 128 MiB of HBM per device.

v0:
```python
import jax
import jax.numpy as jnp
from jax import lax
from jax.experimental import pallas as pl
from jax.experimental.pallas import tpu as pltpu
from jax.sharding import PartitionSpec as P

MESH = pl.DeviceIdType.MESH
F32 = jnp.float32
BF16 = jnp.bfloat16
NY, NZ, NX = 2, 16, 4
CORES = 2


def dot(a, b, dims=((1,), (0,)), precision=None):
    return lax.dot_general(a, b, (dims, ((), ())), precision=precision, preferred_element_type=F32)


def make_kernel(lats, waves, half, degrees):
    nlat = NY * NZ * NX * lats
    zlats = NX * lats
    side = nlat // 2
    width = 2 * half
    peers = NY * NX
    rows = waves // 2
    top = 2 * degrees - 1

    def kernel(
        fourier, legendre, quad_in, slots_in, slots_row, to_in, from_in, rates_in,
        columns, spectral,
        quad, slots_s, slots_v, to_modes, from_modes, rates,
        grid_in, send1, recv1, fold, send2, table_in, table, modes, picks, back,
        updated, parts, recv3, send4, recv4, turned, early,
        local_sem, small_sem, bar_leg, leg_send, spec_sem, spec_send, spec_recv,
        s1, r1, s2, r2, s3, r3, s4, r4, turn,
    ):
        w = lax.axis_index("wave")
        par = lax.axis_index("parity")
        lev = lax.axis_index("lev")
        yl = w // (NZ * NX)
        z = (w // NX) % NZ
        x = w % NX
        sign = (1 - 2 * par).astype(F32)

        def dev(y, zz, xx, q, l):
            return ((y * NZ + zz) * NX + xx, q, l)

        def is_me(d):
            return (d[0] == w) & (d[1] == par) & (d[2] == lev)

        def plane_dst(n):
            q = (par + 1 + n // 8) % 2
            y = (yl + (n // 4) % 2) % 2
            xx = (x + n) % NX
            return y, xx, dev(y, z, xx, q, yl)

        def plane_src(n, l):
            h = (par + 1 + n // NX) % 2
            xx = (x + n) % NX
            return xx, dev(lev, z, xx, h, l)

        def ring(t):
            mag = NZ // 2 - (t + 1) // 2
            return (z + (2 * (t % 2) - 1) * mag + NZ) % NZ

        def signal(d, sem):
            @pl.when(jnp.logical_not(is_me(d)))
            def _():
                pl.semaphore_signal(sem, inc=1, device_id=d, device_id_type=MESH)

        def post(src, dst, send_sem, recv_sem, d):
            me = is_me(d)

            @pl.when(jnp.logical_not(me))
            def _():
                pltpu.make_async_remote_copy(
                    src_ref=src, dst_ref=dst, send_sem=send_sem, recv_sem=recv_sem,
                    device_id=d, device_id_type=MESH,
                ).start()

            @pl.when(me)
            def _():
                pltpu.make_async_copy(src, dst, recv_sem).start()

        def await_bytes(ref, sem):
            pltpu.make_async_copy(ref, ref, sem).wait()

        get_grid = pltpu.make_async_copy(fourier.at[0], grid_in, local_sem.at[0])
        get_grid.start()
        get_leg = pltpu.make_async_copy(
            legendre.at[lev, 0], table.at[pl.ds(lev * side, side)], local_sem.at[1]
        )
        get_leg.start()

        small = [
            pltpu.make_async_copy(src, dst, small_sem.at[n])
            for n, (src, dst) in enumerate((
                (slots_row, slots_v), (quad_in, quad), (slots_in, slots_s),
                (to_in, to_modes), (from_in, from_modes), (rates_in, rates),
            ))
        ]
        for copy in small:
            copy.start()

        barrier = pltpu.get_barrier_semaphore()

        def greet_ring(n, _):
            signal(dev(yl, ring(n // 2), x, par, n % 2), barrier)
            return 0

        def greet_plane(n, _):
            signal(plane_dst(n)[2], barrier)
            signal(plane_src(n // 2, n % 2)[1], barrier)
            return 0

        lax.fori_loop(0, NZ * CORES, greet_ring, 0)
        lax.fori_loop(0, 2 * peers, greet_plane, 0)

        small[0].wait()
        small[1].wait()

        row = lax.broadcasted_iota(jnp.int32, (waves, waves), 0)
        col = lax.broadcasted_iota(jnp.int32, (waves, waves), 1)
        hot = (row == slots_v[...]).astype(F32).astype(BF16)
        zz = row & 15
        xx = (row >> 4) & 3
        yy = (row >> 6) & 1
        ii = row >> 7
        order = (col == (((yy * NZ + zz) * NX + xx) * 2 + ii)).astype(F32).astype(BF16)
        picks[...] = dot(order, hot, ((1,), (1,))).astype(BF16)

        get_grid.wait()
        for pair in range(lats // 2):
            two = [
                (quad[2 * pair + b] * grid_in[2 * pair + b].astype(F32)).astype(BF16)
                for b in range(2)
            ]
            moved = dot(picks[...], jnp.concatenate(two, axis=1)).astype(BF16)
            for i in range(2):
                for b in range(2):
                    block = moved[i * rows : (i + 1) * rows, b * half : (b + 1) * half]
                    send1[i, :, 2 * pair + b] = block.reshape(peers, NZ, half)

        different = (lev != yl).astype(jnp.int32)
        pl.semaphore_wait(barrier, 2 * (2 * peers - 1) + NZ * CORES - 1 + 2 * different)

        def go1(i, first, count, sem):
            def one(n, _):
                y, xx_, d = plane_dst(n)
                post(
                    send1.at[i, y * NX + xx_],
                    recv1.at[i, lev * peers + par * NX + x],
                    s1.at[sem], r1.at[i * 2 + lev], d,
                )
                return 0

            lax.fori_loop(first, first + count, one, 0)

        def pass_on():
            await_bytes(recv1.at[0, pl.ds(0, peers)], s1.at[0])
            pl.semaphore_signal(turn, inc=1, device_id=(w, par, 1 - lev), device_id_type=MESH)

        @pl.when(lev == 0)
        def _():
            go1(0, 0, peers, 0)
            go1(0, peers, peers, 1)
            pass_on()

        @pl.when(lev == 1)
        def _():
            pl.semaphore_wait(turn, 1)
            go1(0, 0, peers, 0)
            go1(0, peers, peers, 1)
            go1(1, 0, 2 * peers, 2)
            pass_on()

        swap = pltpu.make_async_remote_copy(
            src_ref=legendre.at[1 - lev, 0],
            dst_ref=table.at[pl.ds(lev * side, side)],
            send_sem=leg_send.at[0], recv_sem=bar_leg.at[0],
            device_id=(w, par, 1 - lev), device_id_type=MESH,
        )
        swap.start()

        for copy in small[2:]:
            copy.wait()

        into = dot(hot, order, ((1,), (1,)))
        for i in range(2):
            one = into[:, i * rows : (i + 1) * rows]
            back[:, (2 * i) * rows : (2 * i + 1) * rows] = one.astype(BF16)
            back[:, (2 * i + 1) * rows : (2 * i + 2) * rows] = (sign * one).astype(BF16)

        wide_l = lax.broadcasted_iota(jnp.int32, (width, half), 0) >> 1
        spread = (wide_l == lax.broadcasted_iota(jnp.int32, (width, half), 1)).astype(F32)
        same = ((row ^ col) & 1) == 0
        for index, square in enumerate((to_modes, from_modes)):
            tall = dot(spread, square[...], precision=lax.Precision.HIGHEST)
            full = dot(tall, spread, ((1,), (1,)), precision=lax.Precision.HIGHEST)
            modes[index] = jnp.where(same, full, 0.0)
        rates_col = jnp.sum(spread * rates[...], axis=1, keepdims=True)
        eye = (row == col).astype(F32).astype(BF16)

        for chunk in range(4):
            i, l = chunk // 2, chunk % 2
            await_bytes(recv1.at[i, pl.ds(l * peers, peers)], r1.at[chunk])
            for xs in range(NX):
                north = recv1[i, l * peers + xs].astype(F32)
                south = recv1[i, l * peers + NX + xs].astype(F32)
                both = (north + sign * south).reshape(lats * NZ, half)
                fold[xs * lats * NZ : (xs + 1) * lats * NZ, :] = both
            for t in range(NZ):
                send2[chunk, t] = fold[pl.ds(t, zlats, stride=NZ), :].astype(BF16)

            def go2(t, _):
                to = ring(t)
                post(
                    send2.at[chunk, to],
                    table_in.at[l, pl.ds(pl.multiple_of(lev * side + z * zlats, 8), zlats)],
                    s2.at[i], r2.at[l], dev(yl, to, x, par, i),
                )
                return 0

            lax.fori_loop(0, NZ, go2, 0)
            if chunk == 0:

                @pl.when(lev == 0)
                def _():
                    pl.semaphore_wait(turn, 1)
                    go1(1, 0, 2 * peers, 2)

        get_leg.wait()
        swap.wait_recv()
        for l in range(2):
            await_bytes(table_in.at[l], r2.at[l])
            for b in range(nlat // 256):
                turned[l * half : (l + 1) * half, b * 256 : (b + 1) * 256] = dot(
                    eye[:half, :half], table_in[l, b * 256 : (b + 1) * 256, :], ((1,), (1,))
                ).astype(BF16)
        wave = slots_s[2 * w + lev]

        def degrees_step(b, _):
            start = pl.multiple_of(b * 256, 256)
            raw = dot(turned[...], table[:, pl.ds(start, 256)])
            k = lax.broadcasted_iota(jnp.int32, (1, 256), 1) + start
            n = wave + 2 * k + par
            kept = jnp.where(n <= top, raw, 0.0)
            nf = n.astype(F32)
            stiff = nf * (nf + 1.0) / (top * (top + 1.0))
            modal = dot(modes[0], kept, precision=lax.Precision.HIGHEST)
            damped = modal / (1.0 + stiff * rates_col)
            new = dot(modes[1], damped, precision=lax.Precision.HIGHEST).astype(BF16)
            updated[pl.ds(start, 256), :] = dot(eye, new, ((1,), (1,))).astype(BF16)
            return 0

        lax.fori_loop(0, degrees // 256, degrees_step, 0)

        kept_half = degrees // 2
        lanes = pl.ds(pl.multiple_of(lev * width, width), width)
        put_spec = pltpu.make_async_copy(
            updated.at[pl.ds(lev * kept_half, kept_half)], spectral.at[0, :, lanes], spec_sem.at[0]
        )
        put_spec.start()

        def lats_step(b, _):
            start = pl.multiple_of(b * 256, 256)
            new = dot(table[pl.ds(start, 256), :], updated[...]).astype(BF16)
            for l in range(2):
                parts[l, pl.ds(start, 256), :] = new[:, l * half : (l + 1) * half]
            return 0

        lax.fori_loop(0, nlat // 256, lats_step, 0)

        for l in range(2):

            def go3(t, _):
                to = ring(t // 2)
                side_to = t % 2
                post(
                    parts.at[l, pl.ds(pl.multiple_of(side_to * side + to * zlats, 8), zlats)],
                    recv3.at[(lev * 2 + l) * NZ + z],
                    s3.at[0], r3.at[lev * 2 + l], dev(yl, to, x, par, side_to),
                )
                return 0

            lax.fori_loop(0, NZ * CORES, go3, 0)

        swap_spec = pltpu.make_async_remote_copy(
            src_ref=updated.at[pl.ds((1 - lev) * kept_half, kept_half)],
            dst_ref=spectral.at[0, :, lanes],
            send_sem=spec_send.at[0], recv_sem=spec_recv.at[0],
            device_id=(w, par, 1 - lev), device_id_type=MESH,
        )
        swap_spec.start()

        for chunk in range(4):
            i, l = chunk // 2, chunk % 2
            await_bytes(recv3.at[pl.ds(chunk * NZ, NZ)], r3.at[chunk])
            for t in range(NZ):
                fold[t * zlats : (t + 1) * zlats, :] = recv3[chunk * NZ + t].astype(F32)
            for lat in range(zlats):
                picked = fold[pl.ds(lat, NZ, stride=zlats), :]
                send4[chunk, lat // lats, lat % lats] = picked.astype(BF16)

            def go4(n, _):
                xx_, d = plane_src(n, l)
                post(
                    send4.at[chunk, xx_], recv4.at[i, par * peers + yl * NX + x],
                    s4.at[i], r4.at[i], d,
                )
                return 0

            lax.fori_loop(0, peers, go4, 0)

        for i in range(2):
            await_bytes(recv4.at[i], r4.at[i])
            for pair in range(lats // 2):
                cols = [recv4[i, :, 2 * pair + b].reshape(2 * rows, half) for b in range(2)]
                share = dot(
                    back[:, 2 * i * rows : 2 * (i + 1) * rows], jnp.concatenate(cols, axis=1)
                )
                if i == 0:
                    early[pair] = share
                else:
                    both = (early[pair] + share).astype(BF16)
                    for b in range(2):
                        columns[0, 2 * pair + b] = both[:, b * half : (b + 1) * half]

        swap.wait_send()
        swap_spec.wait()
        put_spec.wait()
        await_bytes(recv3.at[pl.ds(0, 2 * NZ * CORES - 2)], s3.at[0])

        def drain(ref, count, sem, has_local):
            @pl.when(has_local)
            def _():
                await_bytes(ref.at[pl.ds(0, count - 1)], sem)

            @pl.when(jnp.logical_not(has_local))
            def _():
                await_bytes(ref.at[pl.ds(0, count)], sem)

        local = lev == yl
        drain(recv1.at[0], peers, s1.at[1], local)
        drain(recv1.at[1], 2 * peers, s1.at[2], local)
        for i in range(2):
            drain(recv4.at[i], 2 * peers, s4.at[i], local)

            @pl.when(lev == i)
            def _():
                await_bytes(recv3.at[pl.ds(0, 2 * NZ - 2)], s2.at[i])

            @pl.when(lev != i)
            def _():
                await_bytes(recv3.at[pl.ds(0, 2 * NZ)], s2.at[i])

    scratch = [
        pltpu.SMEM((lats,), F32),
        pltpu.SMEM((waves,), jnp.int32),
        pltpu.VMEM((1, waves), jnp.int32),
        pltpu.VMEM((half, half), F32),
        pltpu.VMEM((half, half), F32),
        pltpu.VMEM((1, half), F32),
        pltpu.VMEM((lats, waves, half), BF16),
        pltpu.VMEM((2, peers, lats, NZ, half), BF16),
        pltpu.VMEM((2, 2 * peers, lats, NZ, half), BF16),
        pltpu.VMEM((zlats * NZ, half), F32),
        pltpu.VMEM((4, NZ, zlats, half), BF16),
        pltpu.VMEM((2, nlat, half), BF16),
        pltpu.VMEM((nlat, degrees), BF16),
        pltpu.VMEM((2, width, width), F32),
        pltpu.VMEM((waves, waves), BF16),
        pltpu.VMEM((waves, 2 * waves), BF16),
        pltpu.VMEM((degrees, width), BF16),
        pltpu.VMEM((2, nlat, half), BF16),
        pltpu.VMEM((4 * NZ, zlats, half), BF16),
        pltpu.VMEM((4, NX, lats, NZ, half), BF16),
        pltpu.VMEM((2, 2 * peers, lats, NZ, half), BF16),
        pltpu.VMEM((width, nlat), BF16),
        pltpu.VMEM((lats // 2, waves, 2 * half), F32),
        pltpu.SemaphoreType.DMA((2,)),
        pltpu.SemaphoreType.DMA((6,)),
    ] + [pltpu.SemaphoreType.DMA((1,))] * 5 + [
        pltpu.SemaphoreType.DMA((3,)),
        pltpu.SemaphoreType.DMA((4,)),
        pltpu.SemaphoreType.DMA((2,)),
        pltpu.SemaphoreType.DMA((2,)),
        pltpu.SemaphoreType.DMA((1,)),
        pltpu.SemaphoreType.DMA((4,)),
        pltpu.SemaphoreType.DMA((2,)),
        pltpu.SemaphoreType.DMA((2,)),
        pltpu.SemaphoreType.REGULAR,
    ]
    return kernel, scratch


def per_device(fourier, legendre, quad_weights, slot_wave, to_modes, from_modes, mode_rates):
    _, lats, waves, half = fourier.shape
    degrees = legendre.shape[3]
    kernel, scratch = make_kernel(lats, waves, half, degrees)
    vmem = pl.BlockSpec(memory_space=pltpu.VMEM)
    hbm = pl.BlockSpec(memory_space=pltpu.HBM)
    operands = (
        fourier, legendre, quad_weights, slot_wave, slot_wave.reshape(1, waves),
        to_modes, from_modes, mode_rates.reshape(1, half),
    )
    return pl.pallas_call(
        kernel,
        out_shape=(
            jax.ShapeDtypeStruct(fourier.shape, BF16),
            jax.ShapeDtypeStruct((1, degrees // 2, 2 * 2 * half), BF16),
        ),
        in_specs=[hbm] * 8,
        out_specs=(vmem, vmem),
        scratch_shapes=scratch,
        compiler_params=pltpu.CompilerParams(
            collective_id=0, has_side_effects=True, vmem_limit_bytes=48 * 2**20
        ),
    )(*[pltpu.with_memory_space_constraint(v, pltpu.HBM) for v in operands])


def solution(mesh):
    in_specs = (
        P("parity", "wave", None, "lev"),
        P("wave", "parity", "lev", None),
        P("wave"),
        P(),
        P(),
        P(),
        P(),
    )
    out_specs = (P("parity", "wave", None, "lev"), P("parity", "lev", "wave"))
    return jax.shard_map(
        per_device, mesh=mesh, in_specs=in_specs, out_specs=out_specs, check_vma=False
    )
```

profile of v0, /device:TPU:1, one launch (start us, length us, event | category | flops | bytes accessed | tf_op | source)
XLA Modules:
  0.0 98.8 jit_solution(4169698202584914397)
XLA Ops:
  0.6 96.5 %shard_map.86 = (bf16[1,10,256,128]{3,2,1,0:T(8,128)(2,1)S(1)}, bf16[1,640,512]{2,1,0:T(8,128)(2,1)S(1)}) custom-call(bf16[1,10,256,128]{3,2,1,0:T(8,128)(2,1)} %fourier.1, bf16[2,1,640,1280]{3,2,1,0:T(8,128)(2,1)} %legendre.1, f32[10]{0:T(128)} %quad_in.1, s32[256]{0:T(256)} %slots_in.1, s32[1,256]{1,0:T(1,128)} %bitcast.2, f32[128,128]{1,0:T(8,128)} %to_in.1, ...), custom_call_target="tpu_custom_call" | custom-call | tf_op jit(solution)/shard_map/pallas_call | solution.py:407
  97.1 0.8 copy.11
  98.0 0.8 copy.12
where the time goes:
time: 98.9 us; the launch traced here: 98.8 us
  Pallas kernels  96.5 us (98%)
  local copies, waits for them, and re-layouts  1.67 us (2%)
    pallas_call x1, Pallas kernels, per_device(): pl.pallas_call(kernel, out_shape=(jax.ShapeDtypeStruct(fourier.shape, BF1...  96.5 us

commit v1 on v0

--- a/solution.py
+++ b/solution.py
@@ -32,66 +32,65 @@
         grid_in, send1, recv1, fold, send2, table_in, table, modes, picks, back,
         updated, parts, recv3, send4, recv4, turned, early,
         local_sem, small_sem, bar_leg, leg_send, spec_sem, spec_send, spec_recv,
-        s1, r1, s2, r2, s3, r3, s4, r4, turn,
+        s1, r1, s2, r2, s3, r3, s4, r4, turn, known, told,
     ):
         w = lax.axis_index("wave")
         par = lax.axis_index("parity")
         lev = lax.axis_index("lev")
-        yl = w // (NZ * NX)
-        z = (w // NX) % NZ
-        x = w % NX
+        yl = w >> 6
+        z = (w >> 2) & 15
+        x = w & 3
+        local = lev == yl
         sign = (1 - 2 * par).astype(F32)
 
         def dev(y, zz, xx, q, l):
-            return ((y * NZ + zz) * NX + xx, q, l)
-
-        def is_me(d):
-            return (d[0] == w) & (d[1] == par) & (d[2] == lev)
+            return ((y << 6) + (zz << 2) + xx, q, l)
 
         def plane_dst(n):
-            q = (par + 1 + n // 8) % 2
-            y = (yl + (n // 4) % 2) % 2
-            xx = (x + n) % NX
-            return y, xx, dev(y, z, xx, q, yl)
+            q = (par + 1 + (n >> 3)) & 1
+            y = (yl + (n >> 2)) & 1
+            xx = (x + n) & 3
+            return (y << 2) + xx, dev(y, z, xx, q, yl)
 
         def plane_src(n, l):
-            h = (par + 1 + n // NX) % 2
-            xx = (x + n) % NX
+            h = (par + 1 + (n >> 2)) & 1
+            xx = (x + n) & 3
             return xx, dev(lev, z, xx, h, l)
 
         def ring(t):
-            mag = NZ // 2 - (t + 1) // 2
-            return (z + (2 * (t % 2) - 1) * mag + NZ) % NZ
+            away = ((t + 1) >> 1) * (2 * (t & 1) - 1)
+            return (z + 8 + away) & 15
 
         def signal(d, sem):
-            @pl.when(jnp.logical_not(is_me(d)))
-            def _():
-                pl.semaphore_signal(sem, inc=1, device_id=d, device_id_type=MESH)
-
-        def post(src, dst, send_sem, recv_sem, d):
-            me = is_me(d)
-
+            pl.semaphore_signal(sem, inc=1, device_id=d, device_id_type=MESH)
+
+        def send(src, dst, send_sem, recv_sem, d):
+            pltpu.make_async_remote_copy(
+                src_ref=src, dst_ref=dst, send_sem=send_sem, recv_sem=recv_sem,
+                device_id=d, device_id_type=MESH,
+            ).start()
+
+        def post(me, src, dst, send_sem, recv_sem, d):
             @pl.when(jnp.logical_not(me))
             def _():
-                pltpu.make_async_remote_copy(
-                    src_ref=src, dst_ref=dst, send_sem=send_sem, recv_sem=recv_sem,
-                    device_id=d, device_id_type=MESH,
-                ).start()
+                send(src, dst, send_sem, recv_sem, d)
 
             @pl.when(me)
             def _():
                 pltpu.make_async_copy(src, dst, recv_sem).start()
+
+        def loop(first, last, body):
+            def step(n, _):
+                body(n)
+                return 0
+
+            lax.fori_loop(first, last, step, 0)
 
         def await_bytes(ref, sem):
             pltpu.make_async_copy(ref, ref, sem).wait()
 
         get_grid = pltpu.make_async_copy(fourier.at[0], grid_in, local_sem.at[0])
         get_grid.start()
-        get_leg = pltpu.make_async_copy(
-            legendre.at[lev, 0], table.at[pl.ds(lev * side, side)], local_sem.at[1]
-        )
-        get_leg.start()
-
         small = [
             pltpu.make_async_copy(src, dst, small_sem.at[n])
             for n, (src, dst) in enumerate((
@@ -99,22 +98,42 @@
                 (to_in, to_modes), (from_in, from_modes), (rates_in, rates),
             ))
         ]
-        for copy in small:
+        for copy in small[:2]:
             copy.start()
 
         barrier = pltpu.get_barrier_semaphore()
 
-        def greet_ring(n, _):
-            signal(dev(yl, ring(n // 2), x, par, n % 2), barrier)
-            return 0
-
-        def greet_plane(n, _):
-            signal(plane_dst(n)[2], barrier)
-            signal(plane_src(n // 2, n % 2)[1], barrier)
-            return 0
-
-        lax.fori_loop(0, NZ * CORES, greet_ring, 0)
-        lax.fori_loop(0, 2 * peers, greet_plane, 0)
+        def tell(away, sem):
+            for side_to in (-away, away):
+                signal(dev(yl, (z + side_to) & 15, x, par, 0), sem)
+
+        tell(1, barrier)
+
+        def greet_dst(n):
+            signal(plane_dst(n)[1], barrier)
+
+        def greet_src(n):
+            for l in range(2):
+                signal(plane_src(n, l)[1], barrier)
+
+        loop(0, 8, greet_dst)
+        loop(9, 16, greet_dst)
+        loop(0, 4, greet_src)
+        loop(5, 8, greet_src)
+        signal((w, par, 1 - lev), barrier)
+        signal(plane_src(4, 1 - lev)[1], barrier)
+
+        @pl.when(jnp.logical_not(local))
+        def _():
+            signal(plane_dst(8)[1], barrier)
+            signal(plane_src(4, lev)[1], barrier)
+
+        get_leg = pltpu.make_async_copy(
+            legendre.at[lev, 0], table.at[pl.ds(lev * side, side)], local_sem.at[1]
+        )
+        get_leg.start()
+        for copy in small[2:]:
+            copy.start()
 
         small[0].wait()
         small[1].wait()
@@ -129,49 +148,66 @@
         order = (col == (((yy * NZ + zz) * NX + xx) * 2 + ii)).astype(F32).astype(BF16)
         picks[...] = dot(order, hot, ((1,), (1,))).astype(BF16)
 
+        def permute(i):
+            for pair in range(lats // 2):
+                both = jnp.concatenate([grid_in[2 * pair + b] for b in range(2)], axis=1)
+                moved = dot(picks[i * rows : (i + 1) * rows, :], both).astype(BF16)
+                for b in range(2):
+                    block = moved[:, b * half : (b + 1) * half]
+                    send1[i, :, 2 * pair + b] = block.reshape(peers, NZ, half)
+
         get_grid.wait()
-        for pair in range(lats // 2):
-            two = [
-                (quad[2 * pair + b] * grid_in[2 * pair + b].astype(F32)).astype(BF16)
-                for b in range(2)
-            ]
-            moved = dot(picks[...], jnp.concatenate(two, axis=1)).astype(BF16)
-            for i in range(2):
-                for b in range(2):
-                    block = moved[i * rows : (i + 1) * rows, b * half : (b + 1) * half]
-                    send1[i, :, 2 * pair + b] = block.reshape(peers, NZ, half)
+        for lat in range(lats):
+            grid_in[lat] = (quad[lat] * grid_in[lat].astype(F32)).astype(BF16)
+        permute(0)
 
         different = (lev != yl).astype(jnp.int32)
-        pl.semaphore_wait(barrier, 2 * (2 * peers - 1) + NZ * CORES - 1 + 2 * different)
-
-        def go1(i, first, count, sem):
-            def one(n, _):
-                y, xx_, d = plane_dst(n)
-                post(
-                    send1.at[i, y * NX + xx_],
-                    recv1.at[i, lev * peers + par * NX + x],
-                    s1.at[sem], r1.at[i * 2 + lev], d,
-                )
-                return 0
-
-            lax.fori_loop(first, first + count, one, 0)
+        first = (lev == 0).astype(jnp.int32)
+        pl.semaphore_wait(barrier, 2 * (2 * peers - 1) + 1 + 2 * different + 4 * first)
+
+        def go1(i, far, near):
+            def parts_of(n):
+                p, d = plane_dst(n)
+                return send1.at[i, p], recv1.at[i, lev * peers + par * NX + x], d
+
+            def one(sem):
+                def body(n):
+                    src, dst, d = parts_of(n)
+                    send(src, dst, s1.at[sem], r1.at[i * 2 + lev], d)
+
+                return body
+
+            loop(0, 8, one(far))
+            loop(9, 16, one(near))
+            src, dst, d = parts_of(8)
+            post(local, src, dst, s1.at[near], r1.at[i * 2 + lev], d)
 
         def pass_on():
             await_bytes(recv1.at[0, pl.ds(0, peers)], s1.at[0])
-            pl.semaphore_signal(turn, inc=1, device_id=(w, par, 1 - lev), device_id_type=MESH)
+            signal((w, par, 1 - lev), turn)
 
         @pl.when(lev == 0)
         def _():
-            go1(0, 0, peers, 0)
-            go1(0, peers, peers, 1)
+            tell(1, known.at[0])
+            go1(0, 0, 1)
+            pl.semaphore_wait(known.at[0], 2)
+            tell(2, known.at[1])
+
+        permute(1)
+
+        @pl.when(lev == 0)
+        def _():
             pass_on()
+            pl.semaphore_wait(known.at[1], 2)
+            tell(4, known.at[2])
+            pl.semaphore_wait(known.at[2], 2)
+            signal((w, par, 1), told)
 
         @pl.when(lev == 1)
         def _():
             pl.semaphore_wait(turn, 1)
-            go1(0, 0, peers, 0)
-            go1(0, peers, peers, 1)
-            go1(1, 0, 2 * peers, 2)
+            go1(0, 0, 1)
+            go1(1, 2, 2)
             pass_on()
 
         swap = pltpu.make_async_remote_copy(
@@ -197,7 +233,10 @@
         for index, square in enumerate((to_modes, from_modes)):
             tall = dot(spread, square[...], precision=lax.Precision.HIGHEST)
             full = dot(tall, spread, ((1,), (1,)), precision=lax.Precision.HIGHEST)
-            modes[index] = jnp.where(same, full, 0.0)
+            full = jnp.where(same, full, 0.0)
+            high = full.astype(BF16)
+            low = (full - high.astype(F32)).astype(BF16)
+            modes[index] = jnp.concatenate([high, high, low], axis=1)
         rates_col = jnp.sum(spread * rates[...], axis=1, keepdims=True)
         eye = (row == col).astype(F32).astype(BF16)
 
@@ -212,22 +251,32 @@
             for t in range(NZ):
                 send2[chunk, t] = fold[pl.ds(t, zlats, stride=NZ), :].astype(BF16)
 
-            def go2(t, _):
+            if chunk == 0:
+
+                @pl.when(lev == 1)
+                def _():
+                    pl.semaphore_wait(told, 1)
+
+            mine = pl.ds(pl.multiple_of(lev * side + z * zlats, 8), zlats)
+
+            def go2(t):
                 to = ring(t)
-                post(
-                    send2.at[chunk, to],
-                    table_in.at[l, pl.ds(pl.multiple_of(lev * side + z * zlats, 8), zlats)],
-                    s2.at[i], r2.at[l], dev(yl, to, x, par, i),
+                send(
+                    send2.at[chunk, to], table_in.at[l, mine], s2.at[i], r2.at[l],
+                    dev(yl, to, x, par, i),
                 )
-                return 0
-
-            lax.fori_loop(0, NZ, go2, 0)
+
+            loop(0, NZ - 1, go2)
+            post(
+                lev == i, send2.at[chunk, z], table_in.at[l, mine], s2.at[i], r2.at[l],
+                (w, par, i),
+            )
             if chunk == 0:
 
                 @pl.when(lev == 0)
                 def _():
                     pl.semaphore_wait(turn, 1)
-                    go1(1, 0, 2 * peers, 2)
+                    go1(1, 2, 2)
 
         get_leg.wait()
         swap.wait_recv()
@@ -239,21 +288,21 @@
                 ).astype(BF16)
         wave = slots_s[2 * w + lev]
 
-        def degrees_step(b, _):
-            start = pl.multiple_of(b * 256, 256)
-            raw = dot(turned[...], table[:, pl.ds(start, 256)])
+        def mix(index, value):
+            high = value.astype(BF16)
+            low = (value - high.astype(F32)).astype(BF16)
+            return dot(modes[index], jnp.concatenate([high, low, high], axis=0))
+
+        for start in range(0, degrees, 256):
+            raw = dot(turned[...], table[:, start : start + 256])
             k = lax.broadcasted_iota(jnp.int32, (1, 256), 1) + start
             n = wave + 2 * k + par
             kept = jnp.where(n <= top, raw, 0.0)
             nf = n.astype(F32)
             stiff = nf * (nf + 1.0) / (top * (top + 1.0))
-            modal = dot(modes[0], kept, precision=lax.Precision.HIGHEST)
-            damped = modal / (1.0 + stiff * rates_col)
-            new = dot(modes[1], damped, precision=lax.Precision.HIGHEST).astype(BF16)
-            updated[pl.ds(start, 256), :] = dot(eye, new, ((1,), (1,))).astype(BF16)
-            return 0
-
-        lax.fori_loop(0, degrees // 256, degrees_step, 0)
+            damped = mix(0, kept) / (1.0 + stiff * rates_col)
+            new = mix(1, damped).astype(BF16)
+            updated[start : start + 256, :] = dot(eye, new, ((1,), (1,))).astype(BF16)
 
         kept_half = degrees // 2
         lanes = pl.ds(pl.multiple_of(lev * width, width), width)
@@ -262,28 +311,32 @@
         )
         put_spec.start()
 
-        def lats_step(b, _):
-            start = pl.multiple_of(b * 256, 256)
-            new = dot(table[pl.ds(start, 256), :], updated[...]).astype(BF16)
+        for start in range(0, nlat, 256):
+            new = dot(table[start : start + 256, :], updated[...]).astype(BF16)
             for l in range(2):
-                parts[l, pl.ds(start, 256), :] = new[:, l * half : (l + 1) * half]
-            return 0
-
-        lax.fori_loop(0, nlat // 256, lats_step, 0)
+                parts[l, start : start + 256, :] = new[:, l * half : (l + 1) * half]
 
         for l in range(2):
 
-            def go3(t, _):
-                to = ring(t // 2)
-                side_to = t % 2
-                post(
-                    parts.at[l, pl.ds(pl.multiple_of(side_to * side + to * zlats, 8), zlats)],
-                    recv3.at[(lev * 2 + l) * NZ + z],
-                    s3.at[0], r3.at[lev * 2 + l], dev(yl, to, x, par, side_to),
-                )
-                return 0
-
-            lax.fori_loop(0, NZ * CORES, go3, 0)
+            here = (lev * 2 + l) * NZ + z
+
+            def rows_of(y, zz):
+                return parts.at[l, pl.ds(pl.multiple_of(y * side + zz * zlats, 8), zlats)]
+
+            def go3(t):
+                to = ring(t)
+                for y in range(2):
+                    send(
+                        rows_of(y, to), recv3.at[here], s3.at[0], r3.at[lev * 2 + l],
+                        dev(yl, to, x, par, y),
+                    )
+
+            loop(0, NZ - 1, go3)
+            send(
+                rows_of(1 - lev, z), recv3.at[here], s3.at[0], r3.at[lev * 2 + l],
+                (w, par, 1 - lev),
+            )
+            pltpu.make_async_copy(rows_of(lev, z), recv3.at[here], r3.at[lev * 2 + l]).start()
 
         swap_spec = pltpu.make_async_remote_copy(
             src_ref=updated.at[pl.ds((1 - lev) * kept_half, kept_half)],
@@ -302,15 +355,20 @@
                 picked = fold[pl.ds(lat, NZ, stride=zlats), :]
                 send4[chunk, lat // lats, lat % lats] = picked.astype(BF16)
 
-            def go4(n, _):
-                xx_, d = plane_src(n, l)
-                post(
-                    send4.at[chunk, xx_], recv4.at[i, par * peers + yl * NX + x],
+            def go4(n):
+                xx, d = plane_src(n, l)
+                send(
+                    send4.at[chunk, xx], recv4.at[i, par * peers + (yl << 2) + x],
                     s4.at[i], r4.at[i], d,
                 )
-                return 0
-
-            lax.fori_loop(0, peers, go4, 0)
+
+            loop(0, 4, go4)
+            loop(5, 8, go4)
+            xx, d = plane_src(4, l)
+            post(
+                local & (lev == l), send4.at[chunk, xx],
+                recv4.at[i, par * peers + (yl << 2) + x], s4.at[i], r4.at[i], d,
+            )
 
         for i in range(2):
             await_bytes(recv4.at[i], r4.at[i])
@@ -340,7 +398,6 @@
             def _():
                 await_bytes(ref.at[pl.ds(0, count)], sem)
 
-        local = lev == yl
         drain(recv1.at[0], peers, s1.at[1], local)
         drain(recv1.at[1], 2 * peers, s1.at[2], local)
         for i in range(2):
@@ -368,7 +425,7 @@
         pltpu.VMEM((4, NZ, zlats, half), BF16),
         pltpu.VMEM((2, nlat, half), BF16),
         pltpu.VMEM((nlat, degrees), BF16),
-        pltpu.VMEM((2, width, width), F32),
+        pltpu.VMEM((2, width, 3 * width), BF16),
         pltpu.VMEM((waves, waves), BF16),
         pltpu.VMEM((waves, 2 * waves), BF16),
         pltpu.VMEM((degrees, width), BF16),
@@ -389,6 +446,8 @@
         pltpu.SemaphoreType.DMA((4,)),
         pltpu.SemaphoreType.DMA((2,)),
         pltpu.SemaphoreType.DMA((2,)),
+        pltpu.SemaphoreType.REGULAR,
+        pltpu.SemaphoreType.REGULAR((3,)),
         pltpu.SemaphoreType.REGULAR,
     ]
     return kernel, scratch

time: 98.9 us -> 93.5 us (0.945)
  Pallas kernels: 96.5 us -> 91 us
    pallas_call x1, Pallas kernels: 96.5 us -> 91 us  [per_device(): pl.pallas_call(kernel, out_shape=(jax.ShapeDtypeStruct(fourier.shape, BF1...]
where the time goes in v1:
time: 93.5 us; the launch traced here: 93.3 us
  Pallas kernels  91 us (97%)
  local copies, waits for them, and re-layouts  1.67 us (2%)
    pallas_call x1, Pallas kernels, per_device(): pl.pallas_call(kernel, out_shape=(jax.ShapeDtypeStruct(fourier.shape, BF1...  91 us

profile of v1, /device:TPU:1, one launch (start us, length us, event | category | flops | bytes accessed | tf_op | source)
XLA Modules:
  0.0 93.3 jit_solution(9443244231460851342)
XLA Ops:
  0.6 91.0 %shard_map.86 = (bf16[1,10,256,128]{3,2,1,0:T(8,128)(2,1)S(1)}, bf16[1,640,512]{2,1,0:T(8,128)(2,1)S(1)}) custom-call(bf16[1,10,256,128]{3,2,1,0:T(8,128)(2,1)} %fourier.1, bf16[2,1,640,1280]{3,2,1,0:T(8,128)(2,1)} %legendre.1, f32[10]{0:T(128)} %quad_in.1, s32[256]{0:T(256)} %slots_in.1, s32[1,256]{1,0:T(1,128)} %bitcast.2, f32[128,128]{1,0:T(8,128)} %to_in.1, ...), custom_call_target="tpu_custom_call" | custom-call | tf_op jit(solution)/shard_map/pallas_call | solution.py:466
  91.6 0.8 copy.11
  92.5 0.8 copy.12

commit v2 on v1

--- a/solution.py
+++ b/solution.py
@@ -49,16 +49,16 @@
         def plane_dst(n):
             q = (par + 1 + (n >> 3)) & 1
             y = (yl + (n >> 2)) & 1
-            xx = (x + n) & 3
+            xx = (x + n * (1 - 2 * lev)) & 3
             return (y << 2) + xx, dev(y, z, xx, q, yl)
 
         def plane_src(n, l):
             h = (par + 1 + (n >> 2)) & 1
-            xx = (x + n) & 3
+            xx = (x + n * (1 - 2 * lev)) & 3
             return xx, dev(lev, z, xx, h, l)
 
         def ring(t):
-            away = ((t + 1) >> 1) * (2 * (t & 1) - 1)
+            away = ((t + 1) >> 1) * ((2 * (t & 1) - 1) * (1 - 2 * lev))
             return (z + 8 + away) & 15
 
         def signal(d, sem):
@@ -108,6 +108,7 @@
                 signal(dev(yl, (z + side_to) & 15, x, par, 0), sem)
 
         tell(1, barrier)
+        tell(2, barrier)
 
         def greet_dst(n):
             signal(plane_dst(n)[1], barrier)
@@ -163,7 +164,7 @@
 
         different = (lev != yl).astype(jnp.int32)
         first = (lev == 0).astype(jnp.int32)
-        pl.semaphore_wait(barrier, 2 * (2 * peers - 1) + 1 + 2 * different + 4 * first)
+        pl.semaphore_wait(barrier, 2 * (2 * peers - 1) + 1 + 2 * different + 8 * first)
 
         def go1(i, far, near):
             def parts_of(n):
@@ -188,10 +189,10 @@
 
         @pl.when(lev == 0)
         def _():
-            tell(1, known.at[0])
+            tell(2, known.at[0])
             go1(0, 0, 1)
             pl.semaphore_wait(known.at[0], 2)
-            tell(2, known.at[1])
+            tell(4, known.at[1])
 
         permute(1)
 
@@ -199,8 +200,6 @@
         def _():
             pass_on()
             pl.semaphore_wait(known.at[1], 2)
-            tell(4, known.at[2])
-            pl.semaphore_wait(known.at[2], 2)
             signal((w, par, 1), told)
 
         @pl.when(lev == 1)
@@ -447,7 +446,7 @@
         pltpu.SemaphoreType.DMA((2,)),
         pltpu.SemaphoreType.DMA((2,)),
         pltpu.SemaphoreType.REGULAR,
-        pltpu.SemaphoreType.REGULAR((3,)),
+        pltpu.SemaphoreType.REGULAR((2,)),
         pltpu.SemaphoreType.REGULAR,
     ]
     return kernel, scratch

time: 93.5 us -> 92.7 us (level)
  no operation moved by 1% of the time
where the time goes in v2:
time: 92.7 us; the launch traced here: 92.6 us
  Pallas kernels  90.3 us (97%)
  local copies, waits for them, and re-layouts  1.67 us (2%)
    pallas_call x1, Pallas kernels, per_device(): pl.pallas_call(kernel, out_shape=(jax.ShapeDtypeStruct(fourier.shape, BF1...  90.3 us

profile of v2, /device:TPU:1, one launch (start us, length us, event | category | flops | bytes accessed | tf_op | source)
XLA Modules:
  0.0 92.6 jit_solution(8709965403093697454)
XLA Ops:
  0.6 90.3 %shard_map.86 = (bf16[1,10,256,128]{3,2,1,0:T(8,128)(2,1)S(1)}, bf16[1,640,512]{2,1,0:T(8,128)(2,1)S(1)}) custom-call(bf16[1,10,256,128]{3,2,1,0:T(8,128)(2,1)} %fourier.1, bf16[2,1,640,1280]{3,2,1,0:T(8,128)(2,1)} %legendre.1, f32[10]{0:T(128)} %quad_in.1, s32[256]{0:T(256)} %slots_in.1, s32[1,256]{1,0:T(1,128)} %bitcast.2, f32[128,128]{1,0:T(8,128)} %to_in.1, ...), custom_call_target="tpu_custom_call" | custom-call | tf_op jit(solution)/shard_map/pallas_call | solution.py:465
  90.9 0.8 copy.11
  91.8 0.8 copy.12

commit v3 on v2

--- a/solution.py
+++ b/solution.py
@@ -310,32 +310,28 @@
         )
         put_spec.start()
 
-        for start in range(0, nlat, 256):
-            new = dot(table[start : start + 256, :], updated[...]).astype(BF16)
-            for l in range(2):
-                parts[l, start : start + 256, :] = new[:, l * half : (l + 1) * half]
-
-        for l in range(2):
-
-            here = (lev * 2 + l) * NZ + z
-
-            def rows_of(y, zz):
-                return parts.at[l, pl.ds(pl.multiple_of(y * side + zz * zlats, 8), zlats)]
+        def rows_of(l, y, zz):
+            return parts.at[l, pl.ds(pl.multiple_of(y * side + zz * zlats, 8), zlats)]
+
+        def give(l, y):
+            here = recv3.at[(lev * 2 + l) * NZ + z]
+            arrived = r3.at[lev * 2 + l]
 
             def go3(t):
                 to = ring(t)
-                for y in range(2):
-                    send(
-                        rows_of(y, to), recv3.at[here], s3.at[0], r3.at[lev * 2 + l],
-                        dev(yl, to, x, par, y),
-                    )
+                send(rows_of(l, y, to), here, s3.at[0], arrived, dev(yl, to, x, par, y))
 
             loop(0, NZ - 1, go3)
-            send(
-                rows_of(1 - lev, z), recv3.at[here], s3.at[0], r3.at[lev * 2 + l],
-                (w, par, 1 - lev),
-            )
-            pltpu.make_async_copy(rows_of(lev, z), recv3.at[here], r3.at[lev * 2 + l]).start()
+            post(lev == y, rows_of(l, y, z), here, s3.at[0], arrived, (w, par, y))
+
+        for y in range(2):
+            for start in range(y * side, (y + 1) * side, side // 2):
+                new = dot(table[start : start + side // 2, :], updated[...]).astype(BF16)
+                for l in range(2):
+                    parts[l, start : start + side // 2, :] = new[:, l * half : (l + 1) * half]
+            give(0, y)
+        for y in range(2):
+            give(1, y)
 
         swap_spec = pltpu.make_async_remote_copy(
             src_ref=updated.at[pl.ds((1 - lev) * kept_half, kept_half)],

time: 92.7 us -> 89.7 us (0.968)
  Pallas kernels: 90.3 us -> 87.1 us
    pallas_call x1, Pallas kernels: 90.3 us -> 87.1 us  [per_device(): pl.pallas_call(kernel, out_shape=(jax.ShapeDtypeStruct(fourier.shape, BF1...]
where the time goes in v3:
time: 89.7 us; the launch traced here: 89.4 us
  Pallas kernels  87.1 us (97%)
  local copies, waits for them, and re-layouts  1.67 us (2%)
    pallas_call x1, Pallas kernels, per_device(): pl.pallas_call(kernel, out_shape=(jax.ShapeDtypeStruct(fourier.shape, BF1...  87.1 us

profile of v3, /device:TPU:1, one launch (start us, length us, event | category | flops | bytes accessed | tf_op | source)
XLA Modules:
  0.0 89.4 jit_solution(12758306117991573174)
XLA Ops:
  0.6 87.1 %shard_map.86 = (bf16[1,10,256,128]{3,2,1,0:T(8,128)(2,1)S(1)}, bf16[1,640,512]{2,1,0:T(8,128)(2,1)S(1)}) custom-call(bf16[1,10,256,128]{3,2,1,0:T(8,128)(2,1)} %fourier.1, bf16[2,1,640,1280]{3,2,1,0:T(8,128)(2,1)} %legendre.1, f32[10]{0:T(128)} %quad_in.1, s32[256]{0:T(256)} %slots_in.1, s32[1,256]{1,0:T(1,128)} %bitcast.2, f32[128,128]{1,0:T(8,128)} %to_in.1, ...), custom_call_target="tpu_custom_call" | custom-call | tf_op jit(solution)/shard_map/pallas_call | solution.py:461
  87.8 0.8 copy.11
  88.6 0.8 copy.12
